TPU v7x, 32 devices: a whole 2x2x4 slice. The times are simulated.
32 devices in a mesh: dp: 8 (over z, x), mlp: 4 (over y, core).
Axes of the slice: x: 2, y: 2, z: 4, core: 2. Of those that a mesh axis runs over, the one named last changes fastest.
Arguments:
- tokens: bfloat16 [32768, 768], P(('dp', 'mlp')), may hold values from -6 to 6
- cotangent: bfloat16 [32768, 768], P(('dp', 'mlp')), may hold values from -6 to 6
- vectors: float32 [14, 768], replicated
- vector_moments: float32 [14, 768], replicated, may hold values from 819.2 to 26214.4
- decays: float32 [2], replicated, may hold values from 0.9 to 0.98
- owner: int32 [4, 3], replicated, may hold values from 0 to 7, as said below
- master_slots: float32 [8, 4, 768, 768], P('dp', 'mlp'), as said below
- left_slots: float32 [8, 4, 768, 768], P('dp', 'mlp'), as said below
- right_slots: float32 [8, 4, 768, 768], P('dp', 'mlp'), as said below
- left_roots: float32 [8, 4, 768, 768], P('dp', 'mlp'), as said below
- right_roots: float32 [8, 4, 768, 768], P('dp', 'mlp'), as said below
- grid_height: int32 [128], P(('dp', 'mlp')), may hold values from 8 to 24, as said below
- grid_width: int32 [128], P(('dp', 'mlp')), may hold values from 8 to 24, as said below
- patch_rows: int32 [32768], P(('dp', 'mlp')), may hold values from 0 to 23, as said below
- patch_cols: int32 [32768], P(('dp', 'mlp')), may hold values from 0 to 23, as said below
- segment: int32 [32768], P(('dp', 'mlp')), may hold values from 0 to 3, as said below
Outputs:
- output: bfloat16 [32768, 768], P(('dp', 'mlp'))
- input_grad: float32 [32768, 768], P(('dp', 'mlp'))
- slot_grads: float32 [8, 4, 768, 768], P('dp', 'mlp')
- new_left: float32 [8, 4, 768, 768], P('dp', 'mlp')
- new_right: float32 [8, 4, 768, 768], P('dp', 'mlp')
- new_master: float32 [8, 4, 768, 768], P('dp', 'mlp')
- vector_grads: float32 [14, 768], P(None, 'mlp')
- new_vector_moments: float32 [14, 768], P(None, 'mlp')
- new_vectors: float32 [14, 768], P(None, 'mlp')
Inputs may be any that keep to these rules, and one draw needn't show every extreme that they name: `owner`: the entries of a row differ; block kind 0 of row m is the m-th of the query, key, value and output projections, kind 1 the m-th 768 columns of the up projection, kind 2 the m-th 768 rows of the down projection. `master_slots`: slot (owner[m,k], m) holds block kind k of row m; the other slots are unused. `left_slots`: symmetric and positive definite. `right_slots`: symmetric and positive definite. `left_roots`: symmetric and positive definite. `right_roots`: symmetric and positive definite. `grid_height`: each image is 16 patches along one side; the other sides of one device's images add up to 64. `grid_width`: as grid_height. `patch_rows`: each device's patches hold its images whole, one after another in the order of their numbers, each in raster order. `patch_cols`: as patch_rows. `segment`: never falls within a device's patches.
All inputs are finite; a program needn't handle non-finite values.
Results may differ from a plain program's by a relative error of at most 0.014.
Values may be sent and summed in bfloat16 or wider, within the bound.
A program may use at most 192 MiB of HBM per device.

v0:
```python
import math
import jax
import jax.numpy as jnp
from jax import lax
from jax.sharding import PartitionSpec as P

HEADS = 12
GRID_BASE = 16
NORM_EPSILON = 1e-06
GRAFT_EPSILON = 1e-06
STEP_EPSILON = 1e-08
RATE_MATRIX = 0.04
RATE_VECTOR = 0.02
MASKED_SCORE = -1e30


def layer_norm(values, gain_row, shift_row):
    centred = values - jnp.mean(values, axis=-1, keepdims=True)
    spread = jnp.mean(centred * centred, axis=-1, keepdims=True)
    return centred * lax.rsqrt(spread + NORM_EPSILON) * gain_row + shift_row


def exact_gelu(values):
    return jax.nn.gelu(values, approximate=False)


def rotate_pairs(flat_values, freq_row, rows_pos, cols_pos):
    tokens_here = flat_values.shape[0]
    values = flat_values.reshape(tokens_here, HEADS, -1)
    half_size = values.shape[-1] // 2
    middle = freq_row.shape[0] // 2
    freq_cols = freq_row[:middle].reshape(HEADS, half_size)
    freq_rows = freq_row[middle:].reshape(HEADS, half_size)
    angle_grid = (
        rows_pos[:, None, None] * freq_rows[None] + cols_pos[:, None, None] * freq_cols[None]
    )
    cosine = jnp.cos(angle_grid)
    sine_part = jnp.sin(angle_grid)
    first_half = values[..., :half_size]
    second = values[..., half_size:]
    turned = jnp.concatenate(
        [first_half * cosine - second * sine_part, second * cosine + first_half * sine_part],
        axis=-1,
    )
    return turned.reshape(tokens_here, -1)


def patch_positions(segment_ids, heights_in, widths_in, rows_in, cols_in):
    images_here = heights_in.shape[0]
    matches = segment_ids[:, None] == jnp.arange(images_here, dtype=jnp.int32)[None, :]
    heights = jnp.sum(jnp.where(matches, heights_in[None, :], 0), axis=1).astype(jnp.float32)
    widths = jnp.sum(jnp.where(matches, widths_in[None, :], 0), axis=1).astype(jnp.float32)
    rows_pos = rows_in.astype(jnp.float32) * GRID_BASE / heights
    cols_pos = cols_in.astype(jnp.float32) * GRID_BASE / widths
    return (rows_pos, cols_pos)


def heads_first(flat_values):
    return jnp.swapaxes(flat_values.reshape(flat_values.shape[0], HEADS, -1), 0, 1)


def tokens_first(stacked):
    return jnp.swapaxes(stacked, 0, 1).reshape(stacked.shape[1], -1)


def local(
    tokens,
    cotangent,
    vectors,
    vector_moments,
    decays,
    owner,
    master_slots,
    left_slots,
    right_slots,
    left_roots,
    right_roots,
    grid_height,
    grid_width,
    patch_rows,
    patch_cols,
    segment,
):
    dp_index = lax.axis_index("dp")
    mlp_index = lax.axis_index("mlp")
    groups_mlp = lax.axis_size("mlp")
    model_width = tokens.shape[1]
    rows_here = tokens.shape[0]
    owner_row = jnp.take(owner, mlp_index, axis=0)
    holds_block = owner_row == dp_index
    owned_blocks = jnp.where(holds_block[:, None, None], master_slots[0, 0][None], 0.0)
    blocks = lax.psum(owned_blocks, "dp")
    blocks_low = blocks.astype(jnp.bfloat16)
    up_rows = vectors[8 : 8 + groups_mlp]
    down_bias = vectors[8 + groups_mlp]
    freq_row = vectors[9 + groups_mlp]
    every_block = lax.all_gather(blocks_low[None], "mlp", axis=0, tiled=True)
    attention_weights = every_block[:, 0]
    up_weight = every_block[:, 1]
    down_weight = every_block[:, 2]
    up_bias = up_rows.reshape(-1)
    inputs = tokens.astype(jnp.float32)
    norm_one, norm_one_back = jax.vjp(layer_norm, inputs, vectors[0], vectors[1])
    norm_one_low = norm_one.astype(jnp.bfloat16)
    query_lin = (
        jnp.dot(norm_one_low, attention_weights[0], preferred_element_type=jnp.float32) + vectors[2]
    )
    key_lin = (
        jnp.dot(norm_one_low, attention_weights[1], preferred_element_type=jnp.float32) + vectors[3]
    )
    value_low = (
        jnp.dot(norm_one_low, attention_weights[2], preferred_element_type=jnp.float32) + vectors[4]
    ).astype(jnp.bfloat16)
    rows_pos, cols_pos = patch_positions(segment, grid_height, grid_width, patch_rows, patch_cols)

    def rotary_map(flat_values, freq_values):
        return rotate_pairs(flat_values, freq_values, rows_pos, cols_pos)

    query_rot, query_back = jax.vjp(rotary_map, query_lin, freq_row)
    key_rot, key_back = jax.vjp(rotary_map, key_lin, freq_row)
    query_heads = heads_first(query_rot.astype(jnp.bfloat16))
    key_heads = heads_first(key_rot.astype(jnp.bfloat16))
    value_heads = heads_first(value_low)
    same_image = segment[:, None] == segment[None, :]
    score_scale = 1.0 / math.sqrt(model_width // HEADS)

    def head_scores(query_head, key_head):
        scores = jnp.dot(query_head, key_head.T, preferred_element_type=jnp.float32) * score_scale
        return jnp.where(same_image, scores, MASKED_SCORE)

    def head_forward(pieces):
        query_head, key_head, value_head = pieces
        scores = head_scores(query_head, key_head)
        row_peak = jnp.max(scores, axis=1, keepdims=True)
        exponent = jnp.exp(scores - row_peak)
        row_total = jnp.sum(exponent, axis=1, keepdims=True)
        weights_low = (exponent / row_total).astype(jnp.bfloat16)
        attended = jnp.dot(weights_low, value_head, preferred_element_type=jnp.float32)
        return (attended, (row_peak + jnp.log(row_total))[:, 0])

    attended_heads, log_totals = lax.map(head_forward, (query_heads, key_heads, value_heads))
    attended_low = tokens_first(attended_heads).astype(jnp.bfloat16)
    branch_one = (
        jnp.dot(attended_low, attention_weights[3], preferred_element_type=jnp.float32) + vectors[5]
    )
    middle = inputs + branch_one
    norm_two, norm_two_back = jax.vjp(layer_norm, middle, vectors[6], vectors[7])
    norm_two_low = norm_two.astype(jnp.bfloat16)
    pre_act = (
        jnp.einsum(
            "td,mde->tme", norm_two_low, up_weight, preferred_element_type=jnp.float32
        ).reshape(rows_here, -1)
        + up_bias
    )
    activation, gelu_back = jax.vjp(exact_gelu, pre_act)
    activation_blocks = activation.astype(jnp.bfloat16).reshape(rows_here, groups_mlp, -1)
    branch_two = (
        jnp.einsum(
            "tme,med->td", activation_blocks, down_weight, preferred_element_type=jnp.float32
        )
        + down_bias
    )
    grad_act = jnp.einsum(
        "td,med->tme", cotangent, down_weight, preferred_element_type=jnp.float32
    ).reshape(rows_here, -1)
    grad_down = jnp.einsum(
        "tme,td->med", activation_blocks, cotangent, preferred_element_type=jnp.float32
    )
    grad_pre_blocks = gelu_back(grad_act)[0].astype(jnp.bfloat16).reshape(rows_here, groups_mlp, -1)
    grad_up = jnp.einsum(
        "td,tme->mde", norm_two_low, grad_pre_blocks, preferred_element_type=jnp.float32
    )
    up_grad_rows = jnp.sum(grad_pre_blocks, axis=0, dtype=jnp.float32)
    grad_norm_two = jnp.einsum(
        "tme,mde->td", grad_pre_blocks, up_weight, preferred_element_type=jnp.float32
    )
    output_low = (middle + branch_two).astype(jnp.bfloat16)
    grad_middle_norm, grad_gain_two, grad_shift_two = norm_two_back(grad_norm_two)
    grad_middle = cotangent.astype(jnp.float32) + grad_middle_norm
    grad_branch_low = grad_middle.astype(jnp.bfloat16)
    grad_out_bias = jnp.sum(grad_branch_low, axis=0, dtype=jnp.float32)
    grad_out_weight = jnp.dot(attended_low.T, grad_branch_low, preferred_element_type=jnp.float32)
    grad_attended_low = jnp.dot(
        grad_branch_low, attention_weights[3].T, preferred_element_type=jnp.float32
    ).astype(jnp.bfloat16)

    def head_backward(pieces):
        query_head, key_head, value_head, grad_head, log_total = pieces
        scores = head_scores(query_head, key_head)
        probs = jnp.exp(scores - log_total[:, None])
        grad_probs = jnp.dot(grad_head, value_head.T, preferred_element_type=jnp.float32)
        inner = jnp.sum(probs * grad_probs, axis=1, keepdims=True)
        grad_scores = (probs * (grad_probs - inner)).astype(jnp.bfloat16)
        grad_query = (
            jnp.dot(grad_scores, key_head, preferred_element_type=jnp.float32) * score_scale
        )
        grad_key = (
            jnp.dot(grad_scores.T, query_head, preferred_element_type=jnp.float32) * score_scale
        )
        grad_value = jnp.dot(
            probs.astype(jnp.bfloat16).T, grad_head, preferred_element_type=jnp.float32
        )
        return (grad_query, grad_key, grad_value)

    grad_queries, grad_keys, grad_values = lax.map(
        head_backward,
        (query_heads, key_heads, value_heads, heads_first(grad_attended_low), log_totals),
    )
    grad_query_lin, grad_freq_query = query_back(tokens_first(grad_queries))
    grad_key_lin, grad_freq_key = key_back(tokens_first(grad_keys))
    grad_query_low = grad_query_lin.astype(jnp.bfloat16)
    grad_key_low = grad_key_lin.astype(jnp.bfloat16)
    grad_value_low = tokens_first(grad_values).astype(jnp.bfloat16)
    grad_query_weight = jnp.dot(norm_one_low.T, grad_query_low, preferred_element_type=jnp.float32)
    grad_key_weight = jnp.dot(norm_one_low.T, grad_key_low, preferred_element_type=jnp.float32)
    grad_value_weight = jnp.dot(norm_one_low.T, grad_value_low, preferred_element_type=jnp.float32)
    grad_norm_one = jnp.dot(
        grad_query_low, attention_weights[0].T, preferred_element_type=jnp.float32
    )
    grad_norm_one = grad_norm_one + jnp.dot(
        grad_key_low, attention_weights[1].T, preferred_element_type=jnp.float32
    )
    grad_norm_one = grad_norm_one + jnp.dot(
        grad_value_low, attention_weights[2].T, preferred_element_type=jnp.float32
    )
    grad_input_norm, grad_gain_one, grad_shift_one = norm_one_back(grad_norm_one)
    input_grad = grad_middle + grad_input_norm
    head_rows = jnp.stack(
        [
            grad_gain_one,
            grad_shift_one,
            jnp.sum(grad_query_low, axis=0, dtype=jnp.float32),
            jnp.sum(grad_key_low, axis=0, dtype=jnp.float32),
            jnp.sum(grad_value_low, axis=0, dtype=jnp.float32),
            grad_out_bias,
            grad_gain_two,
            grad_shift_two,
        ]
    )
    tail_rows = jnp.stack(
        [jnp.sum(cotangent, axis=0, dtype=jnp.float32), grad_freq_query + grad_freq_key]
    )
    local_vectors = jnp.concatenate([head_rows, up_grad_rows, tail_rows], axis=0)
    vector_sum = lax.psum(local_vectors, ("dp", "mlp"))
    attention_grads = jnp.stack(
        [grad_query_weight, grad_key_weight, grad_value_weight, grad_out_weight]
    )
    attention_share, up_share, down_share = (
        lax.psum_scatter(
            attention_grads.astype(jnp.bfloat16), "mlp", scatter_dimension=0, tiled=True
        ).astype(jnp.float32),
        lax.psum_scatter(
            grad_up.astype(jnp.bfloat16), "mlp", scatter_dimension=0, tiled=True
        ).astype(jnp.float32),
        lax.psum_scatter(
            grad_down.astype(jnp.bfloat16), "mlp", scatter_dimension=0, tiled=True
        ).astype(jnp.float32),
    )
    grad_stack = jnp.concatenate([attention_share, up_share, down_share], axis=0)
    reduced = lax.psum(grad_stack, "dp")
    block_kind = jnp.sum(jnp.where(holds_block, jnp.arange(3, dtype=jnp.int32), 0))
    owns_block = jnp.any(holds_block)
    gradient = jnp.take(reduced, block_kind, axis=0)
    decay_matrix = decays[0]
    left_old = left_slots[0, 0]
    right_old = right_slots[0, 0]
    master_old = master_slots[0, 0]
    left_next = decay_matrix * left_old + (1.0 - decay_matrix) * jnp.dot(
        gradient, gradient.T, precision=lax.Precision.HIGHEST
    )
    right_next = decay_matrix * right_old + (1.0 - decay_matrix) * jnp.dot(
        gradient.T, gradient, precision=lax.Precision.HIGHEST
    )
    direction = jnp.dot(
        jnp.dot(left_roots[0, 0], gradient, precision=lax.Precision.HIGHEST),
        right_roots[0, 0],
        precision=lax.Precision.HIGHEST,
    )
    normed_step = direction * lax.rsqrt(jnp.mean(direction * direction) + GRAFT_EPSILON)
    master_next = master_old - RATE_MATRIX * normed_step
    slot_grad = jnp.where(owns_block, gradient, 0.0)[None, None]
    left_out = jnp.where(owns_block, left_next, left_old)[None, None]
    right_out = jnp.where(owns_block, right_next, right_old)[None, None]
    master_out = jnp.where(owns_block, master_next, master_old)[None, None]
    share_width = model_width // groups_mlp

    def own_columns(table):
        return lax.dynamic_slice_in_dim(table, mlp_index * share_width, share_width, 1)

    grad_share = own_columns(vector_sum)
    moment_old = own_columns(vector_moments)
    vector_old = own_columns(vectors)
    decay_vector = decays[1]
    moment_next = decay_vector * moment_old + (1.0 - decay_vector) * grad_share * grad_share
    vector_next = vector_old - RATE_VECTOR * grad_share / (jnp.sqrt(moment_next) + STEP_EPSILON)
    return (
        output_low,
        input_grad,
        slot_grad,
        left_out,
        right_out,
        master_out,
        grad_share,
        moment_next,
        vector_next,
    )


def solution(mesh):
    placed = (
        P(("dp", "mlp"), None),
        P(("dp", "mlp"), None),
        P(),
        P(),
        P(),
        P(),
        P("dp", "mlp", None, None),
        P("dp", "mlp", None, None),
        P("dp", "mlp", None, None),
        P("dp", "mlp", None, None),
        P("dp", "mlp", None, None),
        P(("dp", "mlp")),
        P(("dp", "mlp")),
        P(("dp", "mlp")),
        P(("dp", "mlp")),
        P(("dp", "mlp")),
    )
    return jax.shard_map(
        local,
        mesh=mesh,
        in_specs=placed,
        out_specs=(
            P(("dp", "mlp"), None),
            P(("dp", "mlp"), None),
            P("dp", "mlp", None, None),
            P("dp", "mlp", None, None),
            P("dp", "mlp", None, None),
            P("dp", "mlp", None, None),
            P(None, "mlp"),
            P(None, "mlp"),
            P(None, "mlp"),
        ),
        check_vma=False,
    )
```

profile of v0, /device:TPU:0, one launch (start us, length us, event | category | flops | bytes accessed | tf_op | source)
XLA Modules:
  0.0 1202.3 jit_solution(14143546167382789815)
XLA Ops:
  8.8 5.2 broadcast_select_fusion
  14.0 278.3 %all-reduce.12 = bf16[3,768,768]{2,1,0:T(8,128)(2,1)} all-reduce(f32[3,768,768]{2,1,0:T(8,128)} %broadcast_select_fusion), channel_id=1, replica_groups=mesh['dp'=8,'mlp'=4] {'dp'}, use_global_device_ids=true, to_apply=%region_2.3 | all-reduce | flops 1769472 | bytes 10616832 | tf_op jit(solution)/shard_map/psum | solution.py:92
  294.8 2.6 copy.100
  303.2 78.7 %all-gather.3.cloned.1.call-done = bf16[12,768,768]{2,1,0:T(8,128)(2,1)} async-done(((bf16[3,768,768]{2,1,0:T(8,128)(2,1)}), bf16[12,768,768]{2,1,0:T(8,128)(2,1)}) %all-gather.3.cloned.1.call-update) | async-done | bytes 14155792 | tf_op jit(solution)/shard_map/all_gather | solution.py:97
  381.8 4.9 slice_bitcast_fusion.3
  386.7 2.9 convolution_add_fusion
  389.7 3.8 convolution_add_fusion.1
  393.6 7.7 subtract_convert_fusion
  402.5 4.1 copy.102
  409.1 4.1 copy.103
  413.2 4.5 add_convert_fusion.4
  417.7 4.1 copy.101
  421.8 85.7 %while.32 = (s32[]{:T(128)}, bf16[12,1024,64]{1,2,0:T(8,128)(2,1)}, f32[12,1024]{1,0:T(8,128)}, bf16[12,1024,64]{2,1,0:T(8,128)(2,1)}, bf16[12,1024,64]{2,1,0:T(...) while((s32[]{:T(128)}, bf16[12,1024,64]{1,2,0:T(8,128)(2,1)}, ...), condition=%wide.region_8.9_spmd.clone.clone, body=%wide.region_5.8_spmd.clone.sunk.clone | while | flops 284163072 | bytes 13695065 | solution.py:141
  424.6 3.0 fusion.195
  431.7 3.0 fusion.195
  438.9 3.0 fusion.195
  446.0 3.0 fusion.195
  453.2 3.0 fusion.195
  460.3 3.0 fusion.195
  467.4 3.0 fusion.195
  474.6 3.0 fusion.195
  481.7 3.0 fusion.195
  488.9 3.0 fusion.195
  496.0 3.0 fusion.195
  503.1 3.0 fusion.195
  507.5 10.2 fusion.64
  517.7 12.7 %copy.133 = f32[1024,3072]{1,0:T(8,128)} copy(f32[1024,3072]{0,1:T(8,128)} %bitcast.277) | data formatting | bytes 25165824 | tf_op jit(solution)/shard_map/reshape | solution.py:165
  530.3 6.6 copy.105
  537.0 4.0 fusion.140
  544.0 40.9 %convert_reduce_fusion = (f32[3072]{0:T(1024)}, bf16[1024,3072]{1,0:T(8,128)(2,1)}, f32[1024,3072]{1,0:T(8,128)}, f32[1024,3072]{1,0:T(8,128)}) fusion(f32[1024,3072]{1,0:T(8,128)S(1)} %copy-done.14, f32[3072]{0:T(1024)S(1)} %add.236, bf16[3072,768]{1,0:T(8,128)(2,1)} %bitcast.289, f32[1024,768]{0,1:T(8,128)S(1)} %get-tuple-element.370, ...), kind=kOutput, calls=%fused_computation.58 | convolution fusion | flops 5071696896 | bytes 51943424 | tf_op jit(solution)/shard_map/td,mde->tme/dot_general | solution.py:150
  584.9 12.8 %multiply_convert_fusion.1 = bf16[1024,3072]{1,0:T(8,128)(2,1)} fusion(f32[1024,3072]{1,0:T(8,128)} %get-tuple-element.336, f32[1024,3072]{1,0:T(8,128)} %get-tuple-element.371, f32[3072]{0:T(1024)S(1)} %add.236), kind=kLoop, calls=%fused_computation.60 | loop fusion | flops 12582912 | bytes 31469568 | tf_op jit(solution)/shard_map/convert_element_type | solution.py:156
  597.8 8.6 copy.137
  606.4 9.0 convolution_convert_fusion
  618.0 8.8 copy.138
  626.8 9.9 fusion.141
  636.7 3.5 copy.112
  640.2 3.9 multiply_reduce_fusion.1
  647.4 4.4 convolution_convert_fusion.1
  651.8 4.1 copy.113
  655.9 10.4 convert_bitcast_fusion
  667.0 159.3 %while.33 = (s32[]{:T(128)}, f32[12,1024,64]{1,2,0:T(8,128)}, f32[12,1024,64]{1,2,0:T(8,128)}, bf16[12,1024,64]{1,2,0:T(8,128)(2,1)}, bf16[12,1024,64]{2,1,0:T(8...) while((s32[]{:T(128)}, f32[12,1024,64]{1,2,0:T(8,128)}, ...), condition=%wide.region_15.16_spmd.clone.clone, body=%wide.region_13.15_spmd.clone.sunk.clone | while | flops 681704448 | bytes 34112624 | solution.py:205
  669.7 2.6 multiply_reduce_fusion.11
  683.0 2.6 multiply_reduce_fusion.11
  709.5 2.6 multiply_reduce_fusion.11
  722.8 2.6 multiply_reduce_fusion.11
  736.0 2.6 multiply_reduce_fusion.11
  775.8 2.6 multiply_reduce_fusion.11
  826.3 12.0 multiply_add_fusion.1
  840.7 7.8 multiply_add_fusion
  860.6 48.4 %reduce-scatter.4.cloned.1.call-done = bf16[1,768,768]{2,1,0:T(8,128)(2,1)} async-done(((bf16[4,768,768]{2,1,0:T(8,128)(2,1)}), bf16[1,768,768]{2,1,0:T(8,128)(2,1)}) %reduce-scatter.4.cloned.1.call-update) | async-done | bytes 1179664 | tf_op jit(solution)/shard_map/reduce_scatter | solution.py:249
  909.0 5.3 maximum_convert_fusion
  919.4 10.5 fusion.75
  932.5 3.3 fusion.114
  935.8 2.8 fusion.115
  938.6 3.1 fusion.133
  944.2 3.3 convert_reduce_fusion.2
  947.5 3.6 copy.125
  955.9 45.1 %psum.23 = f32[14,768]{1,0:T(8,128)S(1)} all-reduce(f32[14,768]{1,0:T(8,128)S(1)} %concatenate.21), channel_id=1, replica_groups=mesh['dp'=8,'mlp'=4] {'dp','mlp'}, use_global_device_ids=true, to_apply=%region_39.40 | all-reduce | flops 10752 | bytes 86016 | tf_op jit(solution)/shard_map/psum | solution.py:244
  1003.1 143.9 %all-reduce.11.cloned.1.call-done = f32[3,768,768]{2,1,0:T(8,128)} async-done(((f32[3,768,768]{2,1,0:T(8,128)}), f32[3,768,768]{2,1,0:T(8,128)}) %all-reduce.11.cloned.1.call-update) | async-done | bytes 7077904 | tf_op jit(solution)/shard_map/psum | solution.py:260
  1147.1 13.6 %fusion.79 = f32[768,768]{1,0:T(8,128)S(1)} fusion(f32[1,1,768,768]{3,2,1,0:T(8,128)} %param.29, f32[3,768,768]{2,1,0:T(8,128)} %all-reduce.11.cloned.1.call-done, s32[]{:T(128)S(6)} %select_n.95, pred[]{:T(512)S(6)} %and.13), kind=kOutput, calls=%fused_computation.124 | convolution fusion | flops 5436407808 | bytes 7077893 | tf_op jit(solution)/shard_map/dot_general | solution.py:275
  1160.7 8.7 multiply_reduce_fusion.4
  1170.1 5.0 fusion.76
  1177.5 8.9 fusion.84
  1186.4 9.2 fusion.82
  (315 shorter events, 247.0 us)
Async XLA Ops:
  7.2 1153.5 %copy-start = (f32[1,1,768,768]{3,2,1,0:T(8,128)S(1)}, f32[1,1,768,768]{3,2,1,0:T(8,128)}, u32[]{:S(2)}) copy-start(f32[1,1,768,768]{3,2,1,0:T(8,128)} %param.30) | copy-start | bytes 7077892
  7.2 374.6 %all-gather.3.cloned.1.call-start = ((), (), s32[]{:S(2)}) async-start(), calls=%async_computation.7 | async-start | bytes 17694720 | tf_op jit(solution)/shard_map/all_gather | solution.py:97
  292.3 568.3 %reduce-scatter.8.cloned.1.call-start = ((), (), s32[]{:S(2)}) async-start(), calls=%async_computation.5 | async-start | bytes 5898240 | tf_op jit(solution)/shard_map/reduce_scatter | solution.py:255
  292.5 1.1 copy-start.9
  293.7 3.8 copy-start.38
  293.7 4.0 slice-start
  293.7 4.0 copy-start.20
  293.7 4.0 copy-start.53
  293.7 4.0 copy-start.54
  294.8 8.3 copy-start.50
  294.8 8.3 copy-start.51
  297.5 96.0 %copy-start.28 = (f32[12,32]{1,0:T(8,128)}, f32[12,32]{1,0:T(8,128)S(1)}, u32[]{:S(2)}) copy-start(f32[12,32]{1,0:T(8,128)S(1)} %mul.390) | copy-start | bytes 4612
  297.6 95.9 %copy-start.30 = (f32[12,32]{1,0:T(8,128)}, f32[12,32]{1,0:T(8,128)S(1)}, u32[]{:S(2)}) copy-start(f32[12,32]{1,0:T(8,128)S(1)} %mul.385) | copy-start | bytes 4612
  298.4 114.8 %copy-start.40 = (f32[768]{0:T(1024)}, f32[768]{0:T(1024)S(1)}, u32[]{:S(2)}) copy-start(f32[768]{0:T(1024)S(1)} %get-tuple-element.290) | copy-start | bytes 9220
  298.4 114.8 %copy-start.48 = (f32[768]{0:T(1024)}, f32[768]{0:T(1024)S(1)}, u32[]{:S(2)}) copy-start(f32[768]{0:T(1024)S(1)} %get-tuple-element.289) | copy-start | bytes 9220
  300.4 112.8 %copy-start.32 = (f32[1024]{0:T(1024)}, f32[1024]{0:T(1024)S(1)}, u32[]{:S(2)}) copy-start(f32[1024]{0:T(1024)S(1)} %broadcast_multiply_fusion.1) | copy-start | bytes 12292
  302.5 0.6 copy-start.44
  302.5 110.7 %copy-start.42 = (f32[1024]{0:T(1024)}, f32[1024]{0:T(1024)S(1)}, u32[]{:S(2)}) copy-start(f32[1024]{0:T(1024)S(1)} %fusion.118) | copy-start | bytes 12292
  303.1 90.4 %copy-start.34 = (f32[1024]{0:T(1024)}, f32[1024]{0:T(1024)S(1)}, u32[]{:S(2)}) copy-start(f32[1024]{0:T(1024)S(1)} %get-tuple-element.377) | copy-start | bytes 12292
  303.1 90.4 %copy-start.36 = (f32[1024]{0:T(1024)}, f32[1024]{0:T(1024)S(1)}, u32[]{:S(2)}) copy-start(f32[1024]{0:T(1024)S(1)} %get-tuple-element.378) | copy-start | bytes 12292
  381.8 4.9 copy-start.1
  389.7 3.9 copy-start.15
  393.5 7.8 copy-start.17
  537.0 7.0 copy-start.14
  541.0 43.9 %copy-start.4 = (f32[1024,768]{0,1:T(8,128)}, f32[1024,768]{0,1:T(8,128)S(1)}, u32[]{:S(2)}) copy-start(f32[1024,768]{0,1:T(8,128)S(1)} %get-tuple-element.370) | copy-start | bytes 9437188
  615.4 245.2 %reduce-scatter.6.cloned.1.call-start = ((), (), s32[]{:S(2)}) async-start(), calls=%async_computation.4 | async-start | bytes 5898240 | tf_op jit(solution)/shard_map/reduce_scatter | solution.py:252
  640.2 3.9 copy-start.5
  640.2 4.7 copy-start.8
  644.9 1.4 copy-start.12
  645.7 1.7 copy-start.6
  647.4 4.4 copy-start.23
  666.3 0.7 copy-start.21
  666.3 242.7 %reduce-scatter.4.cloned.1.call-start = ((), (), s32[]{:S(2)}) async-start(), calls=%async_computation.3 | async-start | bytes 5898240 | tf_op jit(solution)/shard_map/reduce_scatter | solution.py:249
  667.0 159.3 %copy-start.29 = (f32[12,32]{1,0:T(8,128)S(1)}, f32[12,32]{1,0:T(8,128)}, u32[]{:S(2)}) copy-start(f32[12,32]{1,0:T(8,128)} %copy-done.28) | copy-start | bytes 4612
  667.0 159.3 %copy-start.31 = (f32[12,32]{1,0:T(8,128)S(1)}, f32[12,32]{1,0:T(8,128)}, u32[]{:S(2)}) copy-start(f32[12,32]{1,0:T(8,128)} %copy-done.30) | copy-start | bytes 4612
  667.0 159.3 %copy-start.35 = (f32[1024]{0:T(1024)S(1)}, f32[1024]{0:T(1024)}, u32[]{:S(2)}) copy-start(f32[1024]{0:T(1024)} %copy-done.34) | copy-start | bytes 12292
  667.0 159.3 %copy-start.37 = (f32[1024]{0:T(1024)S(1)}, f32[1024]{0:T(1024)}, u32[]{:S(2)}) copy-start(f32[1024]{0:T(1024)} %copy-done.36) | copy-start | bytes 12292
  826.3 12.3 %copy-start.18 = (f32[12,1024,64]{1,2,0:T(8,128)S(1)}, f32[12,1024,64]{1,2,0:T(8,128)}, u32[]{:S(2)}) copy-start(f32[12,1024,64]{1,2,0:T(8,128)} %get-tuple-element.104) | copy-start | bytes 9437188
  838.3 2.5 copy-start.16
  838.5 17.7 %copy-start.25 = (bf16[1024,12,64]{0,2,1:T(8,128)(2,1)}, bf16[1024,12,64]{0,2,1:T(8,128)(2,1)S(1)}, u32[]{:S(2)}) copy-start(bf16[1024,12,64]{0,2,1:T(8,128)(2,1)S(1)} %get-tuple-element.342) | copy-start | bytes 4718596
  848.6 1.4 copy-start.22
  848.6 1.9 copy-start.24
  850.5 4.1 copy-start.26
  850.5 2.0 copy-start.2
  850.5 2.4 copy-start.10
  850.5 2.4 copy-start.33
  850.5 2.4 copy-start.41
  850.5 2.4 copy-start.43
  850.5 2.4 copy-start.49
  860.3 286.7 %all-reduce.11.cloned.1.call-start = ((), (), s32[]{:S(2)}) async-start(), calls=%async_computation.6 | async-start | bytes 14155776 | tf_op jit(solution)/shard_map/psum | solution.py:260
  914.4 1.9 copy-start.52
  914.4 5.1 copy-start.47
  932.5 3.3 copy-start.27
  935.7 2.8 copy-start.3
  935.8 2.8 copy-start.11
  938.6 3.2 copy-start.45
  941.7 1.9 copy-start.7
  941.8 2.4 copy-start.13
  947.5 5.5 copy-start.46
  951.0 50.0 %copy-start.39 = (f32[14,768]{1,0:T(8,128)S(1)}, f32[14,768]{1,0:T(8,128)}, u32[]{:S(2)}) copy-start(f32[14,768]{1,0:T(8,128)} %param.22) | copy-start | bytes 129028
  1170.1 5.0 copy-start.19
  1175.1 2.4 copy-start.55
  1177.5 8.9 copy-start.56
Sparse Core Ops, SparseCore 0:
  292.4 89.3 all-gather.2
  615.5 47.9 reduce-scatter.7
  666.4 48.3 reduce-scatter.5
  860.4 48.5 reduce-scatter.3
  914.5 232.5 all-reduce.10
where the time goes:
time: 1220 us; the launch traced here: 1200 us
  matrix products  359 us (29%)
  blocking collectives  323 us (26%)
  waiting for transfers between devices  271 us (22%)
  local copies, waits for them, and re-layouts  115 us (9%)
  other arithmetic  115 us (9%)
  between operations  18.4 us (2%)
    psum x1, blocking collectives, local(): blocks = lax.psum(owned_blocks, 'dp')  278 us
    psum x1, waiting for transfers between devices, local(): reduced = lax.psum(grad_stack, 'dp')  144 us
    all_gather x1, waiting for transfers between devices, local(): every_block = lax.all_gather(blocks_low[None], 'mlp', axis=0, tiled=True)  78.7 us
    dot_general x24, matrix products, head_scores(): jnp.dot(query_head, key_head.T, preferred_element_type=jnp.float32)  52.2 us
    reduce_scatter x1, waiting for transfers between devices, local(): lax.psum_scatter(attention_grads.astype(jnp.bfloat16), 'mlp', scatter_dim...  48.4 us
    psum x1, blocking collectives, local(): vector_sum = lax.psum(local_vectors, ('dp', 'mlp'))  45.1 us
    dot_general x1, matrix products, local(): jnp.einsum('td,mde->tme', norm_two_low, up_weight, preferred_element_type...  40.9 us
    dot_general x12, matrix products, head_forward(): jnp.dot(weights_low, value_head, preferred_element_type=jnp.float32)  35.5 us
  transfers between devices with their start and end apart: 5, of which 3 were waited for; matrix products, arithmetic and copies ran while one was open for 24% of the time, Pallas kernels for 0%

commit v1 on v0

--- a/solution.py
+++ b/solution.py
@@ -12,6 +12,18 @@
 RATE_MATRIX = 0.04
 RATE_VECTOR = 0.02
 MASKED_SCORE = -1e30
+
+
+def collect(shard, axis, dim):
+    ways, here, step = (lax.axis_size(axis), lax.axis_index(axis), shard.shape[dim])
+    line, have = (shard, 1)
+    while have < ways:
+        line = jnp.concatenate(
+            [line, lax.ppermute(line, axis, [(d, (d - have) % ways) for d in range(ways)])],
+            axis=dim,
+        )
+        have = 2 * have
+    return jnp.roll(line, here * step, axis=dim)
 
 
 def layer_norm(values, gain_row, shift_row):
@@ -94,7 +106,7 @@
     up_rows = vectors[8 : 8 + groups_mlp]
     down_bias = vectors[8 + groups_mlp]
     freq_row = vectors[9 + groups_mlp]
-    every_block = lax.all_gather(blocks_low[None], "mlp", axis=0, tiled=True)
+    every_block = collect(blocks_low[None], "mlp", 0)
     attention_weights = every_block[:, 0]
     up_weight = every_block[:, 1]
     down_weight = every_block[:, 2]

time: 1220 us -> 1320 us (1.082)
  waiting for transfers between devices: 271 us -> 367 us
  other arithmetic: 115 us -> 155 us
  matrix products: 359 us -> 327 us
    ppermute x0 -> x2, waiting for transfers between devices: none -> 177 us  [collect(): lax.ppermute(line, axis, [(d, (d - have) % ways) for d in range(ways)])]
    all_gather x1 -> x0, waiting for transfers between devices: 78.7 us -> none  [local(): every_block = lax.all_gather(blocks_low[None], 'mlp', axis=0, tiled=True)]
    reduce_sum x0 -> x1, other arithmetic: none -> 34.7 us  [local(): up_grad_rows = jnp.sum(grad_pre_blocks, axis=0, dtype=jnp.float32)]
    dot_general x1, matrix products: 40.9 us -> 8.76 us  [local(): jnp.einsum('td,mde->tme', norm_two_low, up_weight, preferred_element_type...]
    dynamic_update_slice x12, local copies, waits for them, and re-layouts: 16.6 us -> 1 us  [local(): lax.map(head_forward, (query_heads, key_heads, value_heads))]
    unnamed x121 -> x138, local copies, waits for them, and re-layouts: 33.5 us -> 46.9 us
  transfers between devices with their start and end apart: 5 -> 6, of which waited for: 3 -> 4; matrix products, arithmetic and copies ran while one was open for 24% -> 22% of each run, Pallas kernels for 0% -> 0%
where the time goes in v1:
time: 1320 us; the launch traced here: 1300 us
  waiting for transfers between devices  367 us (28%)
  matrix products  327 us (25%)
  blocking collectives  323 us (24%)
  other arithmetic  155 us (12%)
  local copies, waits for them, and re-layouts  110 us (8%)
  between operations  18.6 us (1%)
    psum x1, blocking collectives, local(): blocks = lax.psum(owned_blocks, 'dp')  278 us
    ppermute x2, waiting for transfers between devices, collect(): lax.ppermute(line, axis, [(d, (d - have) % ways) for d in range(ways)])  177 us
    psum x1, waiting for transfers between devices, local(): reduced = lax.psum(grad_stack, 'dp')  144 us
    dot_general x24, matrix products, head_scores(): jnp.dot(query_head, key_head.T, preferred_element_type=jnp.float32)  52.5 us
    unnamed x138, local copies, waits for them, and re-layouts  46.9 us
    reduce_scatter x1, waiting for transfers between devices, local(): lax.psum_scatter(attention_grads.astype(jnp.bfloat16), 'mlp', scatter_dim...  46 us
    psum x1, blocking collectives, local(): vector_sum = lax.psum(local_vectors, ('dp', 'mlp'))  45.2 us
    dot_general x12, matrix products, head_forward(): jnp.dot(weights_low, value_head, preferred_element_type=jnp.float32)  35.5 us
  transfers between devices with their start and end apart: 6, of which 4 were waited for; matrix products, arithmetic and copies ran while one was open for 22% of the time, Pallas kernels for 0%

profile of v1, /device:TPU:0, one launch (start us, length us, event | category | flops | bytes accessed | tf_op | source)
XLA Modules:
  0.0 1304.1 jit_solution(7027752177493846842)
XLA Ops:
  8.8 5.2 broadcast_select_fusion
  14.0 278.3 %all-reduce.12 = bf16[3,768,768]{2,1,0:T(8,128)(2,1)} all-reduce(f32[3,768,768]{2,1,0:T(8,128)} %broadcast_select_fusion), channel_id=1, replica_groups=mesh['dp'=8,'mlp'=4] {'dp'}, use_global_device_ids=true, to_apply=%region_2.3 | all-reduce | flops 1769472 | bytes 10616832 | tf_op jit(solution)/shard_map/psum | solution.py:104
  292.8 39.3 %collective-permute-done = bf16[1,3,768,768]{3,2,0,1:T(8,128)(2,1)S(1)} collective-permute-done((bf16[1,3,768,768]{3,2,0,1:T(8,128)(2,1)}, bf16[1,3,768,768]{3,2,0,1:T(8,128)(2,1)S(1)}, u32[]{:S(2)}, u32[]{:S(2)}) %collective-permute-start) | collective-permute-done | bytes 3538976 | tf_op jit(solution)/shard_map/ppermute | solution.py:22
  332.2 6.8 pad_maximum_fusion
  350.2 4.2 constant_dynamic-update-slice_fusion.5
  356.3 138.0 %collective-permute-done.1 = bf16[2,3,768,768]{3,2,0,1:T(8,128)(2,1)} collective-permute-done((bf16[2,3,768,768]{3,2,0,1:T(8,128)(2,1)}, bf16[2,3,768,768]{3,2,0,1:T(8,128)(2,1)}, u32[]{:S(2)}, u32[]{:S(2)}) %collective-permute-start.1) | collective-permute-done | bytes 7077920 | tf_op jit(solution)/shard_map/ppermute | solution.py:22
  494.3 6.3 constant_dynamic-update-slice_fusion.3
  504.8 6.4 constant_dynamic-update-slice_fusion
  511.2 2.9 convolution_add_fusion.1
  514.1 3.8 convolution_add_fusion
  518.0 7.7 subtract_convert_fusion
  526.9 4.1 copy.74
  533.5 4.1 copy.75
  537.6 4.5 add_convert_fusion.4
  542.1 4.1 copy.73
  546.2 70.6 %while.32 = (s32[]{:T(128)}, bf16[12,1024,64]{1,2,0:T(8,128)(2,1)}, f32[12,1024]{1,0:T(8,128)S(1)}, bf16[12,1024,64]{2,1,0:T(8,128)(2,1)}, bf16[12,1024,64]{2,1,...) while((s32[]{:T(128)}, bf16[12,1024,64]{1,2,0:T(8,128)(2,1)}, ...), condition=%wide.region_8.9_spmd.clone.clone, body=%wide.region_5.8_spmd.clone.sunk.clone | while | flops 284163072 | bytes 13695065 | solution.py:153
  549.2 3.0 fusion.207
  555.1 3.0 fusion.207
  560.9 3.0 fusion.207
  566.8 3.0 fusion.207
  572.7 3.0 fusion.207
  578.5 3.0 fusion.207
  584.4 3.0 fusion.207
  590.3 3.0 fusion.207
  596.2 3.0 fusion.207
  602.0 3.0 fusion.207
  607.9 3.0 fusion.207
  613.8 3.0 fusion.207
  616.9 10.1 fusion.64
  626.9 12.6 copy.103
  639.5 4.7 dynamic-slice_bitcast_fusion.3
  644.2 6.6 copy.76
  650.9 4.0 fusion.152
  655.3 8.8 fusion.138
  664.1 34.7 %convert_reduce_fusion = (f32[3072]{0:T(1024)}, bf16[1024,3072]{1,0:T(8,128)(2,1)}, f32[1024,3072]{1,0:T(8,128)}) fusion(f32[1024,3072]{1,0:T(8,128)S(1)} %bitcast.279, f32[1024,3072]{1,0:T(8,128)} %fusion.138, f32[3072]{0:T(1024)S(1)} %add.248), kind=kLoop, calls=%fused_computation.58 | loop fusion | flops 235926528 | bytes 44064768 | tf_op jit(solution)/shard_map/reduce_sum | solution.py:185
  698.8 12.3 multiply_convert_fusion.1
  711.1 8.6 copy.105
  719.7 9.1 convolution_convert_fusion
  731.5 8.9 copy.106
  740.3 9.8 fusion.153
  750.1 3.6 copy.82
  753.7 4.0 multiply_reduce_fusion.1
  760.9 4.4 convolution_convert_fusion.1
  765.3 4.2 copy.83
  769.5 10.2 convert_bitcast_fusion
  779.9 150.5 %while.33 = (s32[]{:T(128)}, f32[12,1024,64]{1,2,0:T(8,128)}, f32[12,1024,64]{1,2,0:T(8,128)}, bf16[12,1024,64]{1,2,0:T(8,128)(2,1)}, bf16[12,1024,64]{2,1,0:T(8...) while((s32[]{:T(128)}, f32[12,1024,64]{1,2,0:T(8,128)}, ...), condition=%wide.region_15.16_spmd.clone.clone, body=%wide.region_13.15_spmd.clone.sunk.clone | while | flops 681704448 | bytes 34112624 | solution.py:217
  819.4 2.7 multiply_reduce_fusion.11
  930.4 12.0 multiply_add_fusion.1
  944.9 7.8 multiply_add_fusion
  964.8 46.0 %reduce-scatter.4.cloned.1.call-done = bf16[1,768,768]{2,1,0:T(8,128)(2,1)} async-done(((bf16[4,768,768]{2,1,0:T(8,128)(2,1)}), bf16[1,768,768]{2,1,0:T(8,128)(2,1)}) %reduce-scatter.4.cloned.1.call-update) | async-done | bytes 1179664 | tf_op jit(solution)/shard_map/reduce_scatter | solution.py:261
  1010.8 5.4 maximum_convert_fusion
  1021.3 10.4 fusion.75
  1034.3 3.3 fusion.114
  1037.6 2.8 fusion.115
  1040.5 3.2 fusion.145
  1046.1 3.3 convert_reduce_fusion.2
  1049.3 3.6 copy.95
  1057.7 45.2 %psum.23 = f32[14,768]{1,0:T(8,128)S(1)} all-reduce(f32[14,768]{1,0:T(8,128)S(1)} %concatenate.33), channel_id=1, replica_groups=mesh['dp'=8,'mlp'=4] {'dp','mlp'}, use_global_device_ids=true, to_apply=%region_39.40 | all-reduce | flops 10752 | bytes 86016 | tf_op jit(solution)/shard_map/psum | solution.py:256
  1105.0 143.9 %all-reduce.11.cloned.1.call-done = f32[3,768,768]{2,1,0:T(8,128)} async-done(((f32[3,768,768]{2,1,0:T(8,128)}), f32[3,768,768]{2,1,0:T(8,128)}) %all-reduce.11.cloned.1.call-update) | async-done | bytes 7077904 | tf_op jit(solution)/shard_map/psum | solution.py:272
  1248.9 13.6 %fusion.79 = f32[768,768]{1,0:T(8,128)S(1)} fusion(f32[1,1,768,768]{3,2,1,0:T(8,128)} %param.29, f32[3,768,768]{2,1,0:T(8,128)} %all-reduce.11.cloned.1.call-done, s32[]{:T(128)S(6)} %select_n.109, pred[]{:T(512)S(6)} %and.20), kind=kOutput, calls=%fused_computation.126 | convolution fusion | flops 5436407808 | bytes 7077893 | tf_op jit(solution)/shard_map/dot_general | solution.py:287
  1262.5 8.7 multiply_reduce_fusion.4
  1271.9 4.9 fusion.76
  1279.2 8.9 fusion.84
  1288.1 9.2 fusion.82
  (338 shorter events, 242.0 us)
Async XLA Ops:
  7.2 1255.3 %copy-start = (f32[1,1,768,768]{3,2,1,0:T(8,128)S(1)}, f32[1,1,768,768]{3,2,1,0:T(8,128)}, u32[]{:S(2)}) copy-start(f32[1,1,768,768]{3,2,1,0:T(8,128)} %param.30) | copy-start | bytes 7077892
  7.2 957.6 %reduce-scatter.8.cloned.1.call-start = ((), (), s32[]{:S(2)}) async-start(), calls=%async_computation.5 | async-start | bytes 5898240 | tf_op jit(solution)/shard_map/reduce_scatter | solution.py:267
  292.3 39.9 %collective-permute-start = (bf16[1,3,768,768]{3,2,0,1:T(8,128)(2,1)}, bf16[1,3,768,768]{3,2,0,1:T(8,128)(2,1)S(1)}, u32[]{:S(2)}, u32[]{:S(2)}) collective-permute-start(bf16[1,3,768,768]{3,2,0,1:T(8,128)(2,1)} %bitcast.276), channel_id=1, source_target_pairs={{0,3},{1,0},{2,1},{3,2},{4,7},{5,4},{6,5},{7,6},{8,11},{9,8},{10,9... | collective-permute-start | bytes 10616840 | tf_op jit(solution)/shard_map/ppermute | solution.py:22
  332.2 6.8 copy-start.5
  338.9 155.4 %collective-permute-start.1 = (bf16[2,3,768,768]{3,2,0,1:T(8,128)(2,1)}, bf16[2,3,768,768]{3,2,0,1:T(8,128)(2,1)}, u32[]{:S(2)}, u32[]{:S(2)}) collective-permute-start(bf16[2,3,768,768]{3,2,0,1:T(8,128)(2,1)} %pad_maximum_fusion), channel_id=1, source_target_pairs={{0,2},{1,3},{2,0},{3,1},{4,6},{5,7},{6,4},{7,5},{8,10},{9,11},{10,... | collective-permute-start | bytes 21233672 | tf_op jit(solution)/shard_map/ppermute | solution.py:22
  341.2 3.8 copy-start.39
  341.2 4.0 slice-start.5
  341.2 4.0 copy-start.22
  341.2 4.0 copy-start.54
  341.2 4.0 copy-start.55
  342.4 7.7 copy-start.51
  342.4 7.7 copy-start.52
  345.1 172.8 %copy-start.29 = (f32[12,32]{1,0:T(8,128)}, f32[12,32]{1,0:T(8,128)S(1)}, u32[]{:S(2)}) copy-start(f32[12,32]{1,0:T(8,128)S(1)} %mul.390) | copy-start | bytes 4612
  345.2 172.7 %copy-start.31 = (f32[12,32]{1,0:T(8,128)}, f32[12,32]{1,0:T(8,128)S(1)}, u32[]{:S(2)}) copy-start(f32[12,32]{1,0:T(8,128)S(1)} %mul.385) | copy-start | bytes 4612
  346.0 191.6 %copy-start.41 = (f32[768]{0:T(1024)}, f32[768]{0:T(1024)S(1)}, u32[]{:S(2)}) copy-start(f32[768]{0:T(1024)S(1)} %get-tuple-element.264) | copy-start | bytes 9220
  346.0 191.6 %copy-start.49 = (f32[768]{0:T(1024)}, f32[768]{0:T(1024)S(1)}, u32[]{:S(2)}) copy-start(f32[768]{0:T(1024)S(1)} %get-tuple-element.263) | copy-start | bytes 9220
  347.7 190.0 %copy-start.33 = (f32[1024]{0:T(1024)}, f32[1024]{0:T(1024)S(1)}, u32[]{:S(2)}) copy-start(f32[1024]{0:T(1024)S(1)} %broadcast_multiply_fusion.1) | copy-start | bytes 12292
  349.5 188.1 %copy-start.44 = (f32[1024]{0:T(1024)}, f32[1024]{0:T(1024)S(1)}, u32[]{:S(2)}) copy-start(f32[1024]{0:T(1024)S(1)} %fusion.119) | copy-start | bytes 12292
  350.1 167.8 %copy-start.35 = (f32[1024]{0:T(1024)}, f32[1024]{0:T(1024)S(1)}, u32[]{:S(2)}) copy-start(f32[1024]{0:T(1024)S(1)} %get-tuple-element.350) | copy-start | bytes 12292
  350.1 167.8 %copy-start.37 = (f32[1024]{0:T(1024)}, f32[1024]{0:T(1024)S(1)}, u32[]{:S(2)}) copy-start(f32[1024]{0:T(1024)S(1)} %get-tuple-element.351) | copy-start | bytes 12292
  350.2 4.2 copy-start.6
  356.3 144.4 %copy-start.1 = (bf16[3,768,768]{2,1,0:T(8,128)(2,1)S(1)}, bf16[3,768,768]{2,1,0:T(8,128)(2,1)}, u32[]{:S(2)}) copy-start(bf16[3,768,768]{2,1,0:T(8,128)(2,1)} %all-reduce.12) | copy-start | bytes 10616836
  504.8 6.4 copy-start.2
  514.1 3.9 copy-start.19
  517.9 7.8 copy-start.17
  650.9 4.4 slice-start.3
  650.9 4.4 slice-start.4
  654.9 9.2 copy-start.7
  654.9 9.2 slice-start
  655.3 8.8 slice-start.1
  655.3 8.8 slice-start.2
  728.8 236.0 %reduce-scatter.6.cloned.1.call-start = ((), (), s32[]{:S(2)}) async-start(), calls=%async_computation.4 | async-start | bytes 5898240 | tf_op jit(solution)/shard_map/reduce_scatter | solution.py:264
  753.7 4.0 copy-start.8
  753.7 4.8 copy-start.11
  760.9 4.4 copy-start.24
  779.8 231.1 %reduce-scatter.4.cloned.1.call-start = ((), (), s32[]{:S(2)}) async-start(), calls=%async_computation.3 | async-start | bytes 5898240 | tf_op jit(solution)/shard_map/reduce_scatter | solution.py:261
  779.8 150.6 %copy-start.30 = (f32[12,32]{1,0:T(8,128)S(1)}, f32[12,32]{1,0:T(8,128)}, u32[]{:S(2)}) copy-start(f32[12,32]{1,0:T(8,128)} %copy-done.29) | copy-start | bytes 4612
  779.8 150.6 %copy-start.32 = (f32[12,32]{1,0:T(8,128)S(1)}, f32[12,32]{1,0:T(8,128)}, u32[]{:S(2)}) copy-start(f32[12,32]{1,0:T(8,128)} %copy-done.31) | copy-start | bytes 4612
  779.8 150.5 %copy-start.36 = (f32[1024]{0:T(1024)S(1)}, f32[1024]{0:T(1024)}, u32[]{:S(2)}) copy-start(f32[1024]{0:T(1024)} %copy-done.35) | copy-start | bytes 12292
  779.9 150.5 %copy-start.38 = (f32[1024]{0:T(1024)S(1)}, f32[1024]{0:T(1024)}, u32[]{:S(2)}) copy-start(f32[1024]{0:T(1024)} %copy-done.37) | copy-start | bytes 12292
  930.4 12.3 copy-start.20
  942.4 2.5 copy-start.18
  942.6 17.7 %copy-start.26 = (bf16[1024,12,64]{0,2,1:T(8,128)(2,1)}, bf16[1024,12,64]{0,2,1:T(8,128)(2,1)S(1)}, u32[]{:S(2)}) copy-start(bf16[1024,12,64]{0,2,1:T(8,128)(2,1)S(1)} %get-tuple-element.316) | copy-start | bytes 4718596
  954.6 4.1 copy-start.27
  954.6 2.0 copy-start.3
  954.6 2.4 copy-start.13
  954.6 2.4 copy-start.34
  954.6 2.4 copy-start.42
  954.6 2.4 copy-start.45
  954.6 2.4 copy-start.50
  964.5 284.4 %all-reduce.11.cloned.1.call-start = ((), (), s32[]{:S(2)}) async-start(), calls=%async_computation.6 | async-start | bytes 14155776 | tf_op jit(solution)/shard_map/psum | solution.py:272
  1016.2 1.9 copy-start.53
  1016.2 5.2 copy-start.48
  1034.3 3.3 copy-start.28
  1037.6 2.8 copy-start.4
  1037.6 2.8 copy-start.14
  1040.4 3.2 copy-start.47
  1043.6 1.9 copy-start.10
  1043.6 2.4 copy-start.16
  1049.3 5.5 copy-start.43
  1052.9 50.0 %copy-start.40 = (f32[14,768]{1,0:T(8,128)S(1)}, f32[14,768]{1,0:T(8,128)}, u32[]{:S(2)}) copy-start(f32[14,768]{1,0:T(8,128)} %param.22) | copy-start | bytes 129028
  1271.9 4.9 copy-start.21
  1276.9 2.3 copy-start.56
  1279.2 8.9 copy-start.57
  (6 other events, 8.1 us)
Sparse Core Ops, SparseCore 0:
  728.9 45.8 reduce-scatter.7
  779.9 46.0 reduce-scatter.5
  964.6 46.1 reduce-scatter.3
  1016.3 232.5 all-reduce.10
